TPU v7x, 32 devices: a whole 2x2x4 slice. The times are simulated.
32 devices in a mesh: abl: 2 (over y), head: 4 (over x, core), ctx: 4 (over z).
Axes of the slice: x: 2, y: 2, z: 4, core: 2. Of those that a mesh axis runs over, the one named last changes fastest.
Arguments:
- queries: bfloat16 [1024, 6144], P(('abl', 'head', 'ctx')), parts along dimension 0, may hold values from -30 to 30
- keys: bfloat16 [16384, 6144], P(('abl', 'ctx'), 'head'), parts along dimension 0, may hold values from -6 to 6
- values: bfloat16 [16384, 6144], P(('abl', 'ctx'), 'head'), parts along dimension 0, may hold values from -6 to 6
- kept_rows: int32 [128], P(('abl', 'ctx')), parts along dimension 0, may hold values from 0 to 1, as said below
- out_weight: bfloat16 [6144, 6144], P('head'), may hold values from -6 to 6
Outputs:
- projected: bfloat16 [1024, 6144], P(('abl', 'head', 'ctx')), parts along dimension 0
There are 2 independent parts, one for each index of `abl`. A program takes and returns all parts, laid end to end along the dimension named above; an argument that names none is the same for every part. Nothing has to cross between parts.
Inputs may be any that keep to these rules, and one draw needn't show every extreme that they name: `kept_rows`: in every part the first row of each block of 16 consecutive rows is kept.
All inputs are finite; a program needn't handle non-finite values.
Results may differ from a plain program's by a relative error of at most 0.028.
Values may be sent and summed in bfloat16 or wider, within the bound.
No kernel may reach another device: no remote copies, remote signals or barrier semaphores. Data moves between devices by JAX's collectives and lax.ppermute only.
A program may use at most 128 MiB of HBM per device.

v0:
```python
import math
import jax
import jax.numpy as jnp
from jax import lax
from jax.sharding import PartitionSpec as P

HD = 128


def shards(queries, keys, values, kept_rows, out_weight):
    score_scale = 1.0 / math.sqrt(HD)
    local_heads = keys.shape[1] // HD
    key_count = keys.shape[0]
    key_heads = keys.reshape(key_count, local_heads, HD)
    value_heads = values.reshape(key_count, local_heads, HD)
    visible = jnp.repeat(kept_rows, 128) > 0
    query_block = lax.all_to_all(queries, "head", split_axis=1, concat_axis=0, tiled=True)
    all_queries = lax.all_gather(query_block, "ctx", axis=0, tiled=True)
    row_count = all_queries.shape[0]
    zeros_sum = jnp.zeros((row_count, local_heads * HD), jnp.float32)
    lowest = jnp.full((local_heads, row_count), -1e30, jnp.float32)
    summed = zeros_sum
    row_count = all_queries.shape[0]
    shaped = all_queries.reshape(row_count, local_heads, HD)
    scores = (
        jnp.einsum("qhd,khd->hqk", shaped, key_heads, preferred_element_type=jnp.float32)
        * score_scale
    )
    scores = jnp.where(visible[None, None, :], scores, -jnp.inf)
    highest = jnp.maximum(lowest, jnp.max(scores, axis=-1))
    rescale = jnp.exp(lowest - highest)
    softened = jnp.exp(scores - highest[..., None])
    normal_sum = jnp.sum(softened, axis=-1)
    mixed = jnp.einsum(
        "hqk,khd->qhd",
        softened.astype(jnp.bfloat16),
        value_heads,
        preferred_element_type=jnp.float32,
    )
    summed = summed * jnp.repeat(rescale.T, HD, axis=1) + mixed.reshape(row_count, local_heads * HD)
    summed, running, normal_sum = (summed, highest, normal_sum)
    highest = lax.pmax(running, "ctx")
    rescale = jnp.exp(running - highest)
    summed = summed * jnp.repeat(rescale.T, HD, axis=1)
    normal_sum = normal_sum * rescale
    summed, normal_sum = (
        lax.psum_scatter(
            summed.astype(jnp.bfloat16), "ctx", scatter_dimension=0, tiled=True
        ).astype(jnp.float32),
        lax.psum_scatter(
            normal_sum.astype(jnp.bfloat16), "ctx", scatter_dimension=1, tiled=True
        ).astype(jnp.float32),
    )
    attended = (summed / jnp.repeat(normal_sum.T, HD, axis=1)).astype(jnp.bfloat16)
    return lax.psum_scatter(
        jnp.dot(attended, out_weight, preferred_element_type=jnp.float32).astype(jnp.bfloat16),
        "head",
        scatter_dimension=0,
        tiled=True,
    )


def solution(mesh):
    placed = (
        P(("abl", "head", "ctx"), None),
        P(("abl", "ctx"), "head"),
        P(("abl", "ctx"), "head"),
        P(("abl", "ctx")),
        P("head", None),
    )
    return jax.shard_map(
        shards,
        mesh=mesh,
        in_specs=placed,
        out_specs=P(("abl", "head", "ctx"), None),
        check_vma=False,
    )
```

profile of v0, /device:TPU:0, one launch (start us, length us, event | category | flops | bytes accessed | tf_op | source)
XLA Modules:
  0.0 223.1 jit_solution(14071060724346164999)
XLA Ops:
  6.5 0.0 copy-start
  6.5 0.0 all-gather.2.cloned.1.call-start
  6.5 1.0 copy.33
  7.6 11.6 %all_to_all.19 = bf16[32,4,1536]{2,0,1:T(8,128)(2,1)} all-to-all(bf16[32,4,1536]{2,0,1:T(8,128)(2,1)S(1)} %bitcast.42), channel_id=1, replica_groups=mesh['abl'=2,'head'=4,'ctx'=4] {'head'}, dimensions={1} | all-to-all | bytes 786432 | tf_op jit(solution)/shard_map/all_to_all | solution.py:17
  19.1 0.0 all-gather.2.cloned.1.call-update
  19.2 0.0 reduce-scatter.12.cloned.1.call-start
  19.2 8.8 %copy.21 = bf16[2048,1536]{0,1:T(8,128)(2,1)} copy(bf16[2048,1536]{1,0:T(8,128)(2,1)} %param.6) | data formatting | bytes 12582912 | tf_op args[1]
  28.0 8.8 %copy.24 = bf16[2048,1536]{0,1:T(8,128)(2,1)} copy(bf16[2048,1536]{1,0:T(8,128)(2,1)} %param.7) | data formatting | bytes 12582912 | tf_op args[2]
  36.7 0.0 copy-done
  36.7 0.1 broadcast_bitcast_fusion
  36.8 20.3 %all-gather.2.cloned.1.call-done = bf16[512,1536]{1,0:T(8,128)(2,1)} async-done(((bf16[128,1536]{1,0:T(8,128)(2,1)}), bf16[512,1536]{1,0:T(8,128)(2,1)}) %all-gather.2.cloned.1.call-update) | async-done | bytes 1572880 | tf_op jit(solution)/shard_map/all_gather | solution.py:18
  57.1 1.7 copy.20
  58.8 22.6 %fusion = (f32[12,512]{1,0:T(8,128)S(1)}, f32[12,512,2048]{2,1,0:T(8,128)}) fusion(pred[2048]{0:T(1024)(128)(4,1)S(1)} %broadcast_bitcast_fusion, bf16[512,12,128]{0,2,1:T(8,128)(2,1)S(1)} %bitcast.38, bf16[2048,12,128]{0,2,1:T(8,128)(2,1)} %bitcast.37), kind=kOutput, calls=%fused_computation.2 | convolution fusion | flops 3258968064 | bytes 58222592 | tf_op jit(solution)/shard_map/qhd,khd->hqk/dot_general | solution.py:26
  81.4 16.9 %pmax.7 = f32[12,512]{1,0:T(8,128)S(1)} all-reduce(f32[12,512]{1,0:T(8,128)S(1)} %broadcast_maximum_fusion), channel_id=1, replica_groups=mesh['abl'=2,'head'=4,'ctx'=4] {'ctx'}, use_global_device_ids=true, to_apply=%region_1.2 | all-reduce | flops 6144 | bytes 49152 | tf_op jit(solution)/shard_map/pmax | solution.py:42
  98.4 21.1 %fusion.1 = f32[12,512]{1,0:T(8,128)S(1)} fusion(f32[12,512,2048]{2,1,0:T(8,128)} %get-tuple-element.9, f32[12,512]{1,0:T(8,128)S(1)} %broadcast_maximum_fusion, pred[2048]{0:T(1024)(128)(4,1)S(1)} %broadcast_bitcast_fusion), kind=kLoop, calls=%fused_computation.3 | loop fusion | flops 50325504 | bytes 50382848 | tf_op jit(solution)/shard_map/reduce_sum | solution.py:33
  119.5 0.8 copy.29
  120.3 0.0 reduce-scatter.12.cloned.1.call-update
  120.3 0.0 reduce-scatter.10.cloned.1.call-start
  120.4 22.0 %fusion.7 = bf16[512,12,128]{0,2,1:T(8,128)(2,1)S(1)} fusion(bf16[2048,12,128]{0,2,1:T(8,128)(2,1)} %bitcast.39, f32[12,512,2048]{2,1,0:T(8,128)} %get-tuple-element.9, f32[12,512]{1,0:T(8,128)S(1)} %broadcast_maximum_fusion, pred[2048]{0:T(1024)(128)(4,1)S(1)} %broadcast_bitcast_fusion, f32[512,12]{0,1:T(8,128)S(1)} %get-tuple-element.6, ...), kind=kOutput, calls=%fused_computation.10 | convolution fusion | flops 3273916416 | bytes 58271744 | tf_op jit(solution)/shard_map/hqk,khd->qhd/dot_general | solution.py:34
  142.4 1.6 copy.27
  144.0 0.0 reduce-scatter.10.cloned.1.call-update
  144.0 0.2 reduce-scatter.8.cloned.1.call-start
  144.2 0.0 reduce-scatter.12.cloned.1.call-done
  144.3 0.8 copy.30
  145.1 32.7 %reduce-scatter.10.cloned.1.call-done = bf16[128,1536]{1,0:T(8,128)(2,1)} async-done(((bf16[512,1536]{1,0:T(8,128)(2,1)}), bf16[128,1536]{1,0:T(8,128)(2,1)}) %reduce-scatter.10.cloned.1.call-update) | async-done | bytes 393232
  177.7 1.2 copy.28
  179.0 0.1 fusion.10
  179.1 10.2 %convolution_convert_fusion = bf16[128,6144]{1,0:T(8,128)(2,1)} fusion(bf16[128,1536]{0,1:T(8,128)(2,1)S(1)} %fusion.10, bf16[1536,6144]{1,0:T(8,128)(2,1)} %param.9), kind=kOutput, calls=%fused_computation.7 | convolution fusion | flops 2416705536 | bytes 20840448 | tf_op jit(solution)/shard_map/dot_general | solution.py:56
  189.3 0.0 reduce-scatter.8.cloned.1.call-update
  189.3 27.3 %reduce-scatter.8.cloned.1.call-done = bf16[32,6144]{1,0:T(8,128)(2,1)} async-done(((bf16[128,6144]{1,0:T(8,128)(2,1)}), bf16[32,6144]{1,0:T(8,128)(2,1)}) %reduce-scatter.8.cloned.1.call-update) | async-done | bytes 393232 | tf_op jit(solution)/shard_map/reduce_scatter | solution.py:55
  (4 shorter events, 0.0 us)
Async XLA Ops:
  6.5 30.2 %copy-start = (s32[16]{0:T(128)S(1)}, s32[16]{0:T(128)}, u32[]{:S(2)}) copy-start(s32[16]{0:T(128)} %param.8) | copy-start | bytes 196
  6.5 50.6 %all-gather.2.cloned.1.call-start = ((), (), s32[]{:S(2)}) async-start(), calls=%async_computation.4 | async-start | bytes 1966080 | tf_op jit(solution)/shard_map/all_gather | solution.py:18
  19.2 125.1 %reduce-scatter.12.cloned.1.call-start = ((), (), s32[]{:S(2)}) async-start(), calls=%async_computation.7 | async-start | bytes 163840
  120.3 57.4 %reduce-scatter.10.cloned.1.call-start = ((), (), s32[]{:S(2)}) async-start(), calls=%async_computation.6 | async-start | bytes 1966080
  144.0 72.6 %reduce-scatter.8.cloned.1.call-start = ((), (), s32[]{:S(2)}) async-start(), calls=%async_computation.5 | async-start | bytes 1966080 | tf_op jit(solution)/shard_map/reduce_scatter | solution.py:55
Sparse Core Ops, SparseCore 0:
  19.3 37.8 all-gather.1
  120.4 17.4 reduce-scatter.11
  144.1 33.5 reduce-scatter.9
  189.4 27.1 reduce-scatter.7
where the time goes:
time: 224 us; the launch traced here: 223 us
  waiting for transfers between devices  80.4 us (36%)
  matrix products  54.9 us (25%)
  blocking collectives  28.5 us (13%)
  local copies, waits for them, and re-layouts  24.7 us (11%)
  other arithmetic  21.2 us (9%)
  between operations  13.2 us (6%)
    unnamed x6, waiting for transfers between devices  32.7 us
    reduce_scatter x1, waiting for transfers between devices, shards(): lax.psum_scatter(jnp.dot(attended, out_weight, preferred_element_type=jnp...  27.3 us
    dot_general x1, matrix products, shards(): jnp.einsum('qhd,khd->hqk', shaped, key_heads, preferred_element_type=jnp....  22.6 us
    dot_general x1, matrix products, shards(): jnp.einsum('hqk,khd->qhd', softened.astype(jnp.bfloat16), value_heads, pr...  22 us
    unnamed x8, local copies, waits for them, and re-layouts  21.9 us
    reduce_sum x1, other arithmetic, shards(): normal_sum = jnp.sum(softened, axis=-1)  21.1 us
    all_gather x1, waiting for transfers between devices, shards(): all_queries = lax.all_gather(query_block, 'ctx', axis=0, tiled=True)  20.3 us
    pmax x1, blocking collectives, shards(): highest = lax.pmax(running, 'ctx')  16.9 us
  transfers between devices with their start and end apart: 4, of which 3 were waited for; matrix products, arithmetic and copies ran while one was open for 19% of the time, Pallas kernels for 0%

commit v1 on v0

--- a/solution.py
+++ b/solution.py
@@ -7,6 +7,18 @@
 HD = 128
 
 
+def split_up(x, dim, size):
+    lengths = x.shape
+    blocks = x.reshape(*lengths[:dim], size, lengths[dim] // size, *lengths[dim + 1 :])
+    return jnp.moveaxis(blocks, dim, 0)
+
+
+def in_order(tiles, dim):
+    shape = list(tiles.shape[1:])
+    shape[dim] *= tiles.shape[0]
+    return jnp.moveaxis(tiles, 0, dim).reshape(shape)
+
+
 def shards(queries, keys, values, kept_rows, out_weight):
     score_scale = 1.0 / math.sqrt(HD)
     local_heads = keys.shape[1] // HD
@@ -14,7 +26,14 @@
     key_heads = keys.reshape(key_count, local_heads, HD)
     value_heads = values.reshape(key_count, local_heads, HD)
     visible = jnp.repeat(kept_rows, 128) > 0
-    query_block = lax.all_to_all(queries, "head", split_axis=1, concat_axis=0, tiled=True)
+    count, position = (lax.axis_size("head"), lax.axis_index("head"))
+    blocks = split_up(queries, 1, count)
+    outs = [blocks[position]]
+    for turn in range(1, count):
+        sent = blocks[position ^ turn]
+        outs.append(lax.ppermute(sent, "head", [(i, i ^ turn) for i in range(count)]))
+    blocks = jnp.stack(outs)[position ^ jnp.arange(count)]
+    query_block = in_order(blocks, 0)
     all_queries = lax.all_gather(query_block, "ctx", axis=0, tiled=True)
     row_count = all_queries.shape[0]
     zeros_sum = jnp.zeros((row_count, local_heads * HD), jnp.float32)

time: 224 us -> 223 us (level)
  blocking collectives: 28.5 us -> 17.3 us
  waiting for transfers between devices: 80.4 us -> 86.3 us
  starting transfers between devices: 0.31 us -> 3.58 us
    all_to_all x1 -> x0, blocking collectives: 11.6 us -> none  [shards(): lax.all_to_all(queries, 'head', split_axis=1, concat_axis=0, tiled=True)]
    ppermute x0 -> x3, waiting for transfers between devices: none -> 5.11 us  [shards(): lax.ppermute(sent, 'head', [(i, i ^ turn) for i in range(count)])]
    ppermute x0 -> x3, starting transfers between devices: none -> 3.27 us  [shards(): lax.ppermute(sent, 'head', [(i, i ^ turn) for i in range(count)])]
    unnamed x8 -> x12, local copies, waits for them, and re-layouts: 21.9 us -> 21.9 us
  transfers between devices with their start and end apart: 4 -> 7, of which waited for: 3 -> 5; matrix products, arithmetic and copies ran while one was open for 19% -> 19% of each run, Pallas kernels for 0% -> 0%
where the time goes in v1:
time: 223 us; the launch traced here: 222 us
  waiting for transfers between devices  86.3 us (39%)
  matrix products  55.1 us (25%)
  local copies, waits for them, and re-layouts  25.6 us (11%)
  other arithmetic  21.3 us (10%)
  blocking collectives  17.3 us (8%)
  between operations  13.3 us (6%)
  starting transfers between devices  3.58 us (2%)
    unnamed x6, waiting for transfers between devices  32.3 us
    reduce_scatter x1, waiting for transfers between devices, shards(): lax.psum_scatter(jnp.dot(attended, out_weight, preferred_element_type=jnp...  27.3 us
    dot_general x1, matrix products, shards(): jnp.einsum('qhd,khd->hqk', shaped, key_heads, preferred_element_type=jnp....  22.8 us
    dot_general x1, matrix products, shards(): jnp.einsum('hqk,khd->qhd', softened.astype(jnp.bfloat16), value_heads, pr...  22 us
    unnamed x12, local copies, waits for them, and re-layouts  21.9 us
    all_gather x1, waiting for transfers between devices, shards(): all_queries = lax.all_gather(query_block, 'ctx', axis=0, tiled=True)  21.6 us
    reduce_sum x1, other arithmetic, shards(): normal_sum = jnp.sum(softened, axis=-1)  21.1 us
    pmax x1, blocking collectives, shards(): highest = lax.pmax(running, 'ctx')  17.3 us
  transfers between devices with their start and end apart: 7, of which 5 were waited for; matrix products, arithmetic and copies ran while one was open for 19% of the time, Pallas kernels for 0%

profile of v1, /device:TPU:0, one launch (start us, length us, event | category | flops | bytes accessed | tf_op | source)
XLA Modules:
  0.0 222.5 jit_solution(8334604792437196144)
XLA Ops:
  6.5 1.3 reshape.62
  7.9 0.8 constant_dynamic-slice_fusion.3
  8.7 0.5 collective-permute-start
  9.2 2.6 %collective-permute-start.1 = (bf16[32,1536]{1,0:T(8,128)(2,1)S(1)}, bf16[32,1536]{1,0:T(8,128)(2,1)S(1)}, u32[]{:S(2)}, u32[]{:S(2)}) collective-permute-start(bf16[32,1536]{1,0:T(8,128)(2,1)S(1)} %bitcast.59), channel_id=1, source_target_pairs={{0,8},{4,12},{8,0},{12,4},{1,9},{5,13},{9,1},{13,5},{2,10},{6,14},... | collective-permute-start | bytes 294920 | tf_op jit(solution)/shard_map/ppermute | solution.py:34
  11.8 0.2 collective-permute-start.2
  12.1 3.4 %collective-permute-done.1 = bf16[32,1536]{1,0:T(8,128)(2,1)S(1)} collective-permute-done((bf16[32,1536]{1,0:T(8,128)(2,1)S(1)}, bf16[32,1536]{1,0:T(8,128)(2,1)S(1)}, u32[]{:S(2)}, u32[]{:S(2)}) %collective-permute-start.1) | collective-permute-done | bytes 98336 | tf_op jit(solution)/shard_map/ppermute | solution.py:34
  15.5 1.7 collective-permute-done.2
  17.2 0.1 pad_maximum_fusion
  17.2 0.6 gather_fusion
  17.8 0.9 copy.18
  18.7 0.0 all-gather.2.cloned.1.call-update
  18.7 0.0 reduce-scatter.12.cloned.1.call-start
  18.8 8.7 %copy.19 = bf16[2048,1536]{0,1:T(8,128)(2,1)} copy(bf16[2048,1536]{1,0:T(8,128)(2,1)} %param.6) | data formatting | bytes 12582912 | tf_op args[1]
  27.5 8.7 %copy.22 = bf16[2048,1536]{0,1:T(8,128)(2,1)} copy(bf16[2048,1536]{1,0:T(8,128)(2,1)} %param.7) | data formatting | bytes 12582912 | tf_op args[2]
  36.2 0.1 broadcast_bitcast_fusion
  36.3 21.6 %all-gather.2.cloned.1.call-done = bf16[512,1536]{0,1:T(8,128)(2,1)} async-done(((bf16[128,1536]{0,1:T(8,128)(2,1)}), bf16[512,1536]{0,1:T(8,128)(2,1)}) %all-gather.2.cloned.1.call-update) | async-done | bytes 1572880 | tf_op jit(solution)/shard_map/all_gather | solution.py:37
  57.9 22.8 %fusion = (f32[12,512]{1,0:T(8,128)S(1)}, f32[12,512,2048]{2,1,0:T(8,128)}) fusion(pred[2048]{0:T(1024)(128)(4,1)S(1)} %broadcast_bitcast_fusion, bf16[512,12,128]{0,2,1:T(8,128)(2,1)} %bitcast.50, bf16[2048,12,128]{0,2,1:T(8,128)(2,1)} %bitcast.48), kind=kOutput, calls=%fused_computation.3 | convolution fusion | flops 3258968064 | bytes 58222592 | tf_op jit(solution)/shard_map/qhd,khd->hqk/dot_general | solution.py:45
  80.7 17.3 %pmax.7 = f32[12,512]{1,0:T(8,128)S(1)} all-reduce(f32[12,512]{1,0:T(8,128)S(1)} %broadcast_maximum_fusion), channel_id=1, replica_groups=mesh['abl'=2,'head'=4,'ctx'=4] {'ctx'}, use_global_device_ids=true, to_apply=%region_1.2 | all-reduce | flops 6144 | bytes 49152 | tf_op jit(solution)/shard_map/pmax | solution.py:61
  98.1 21.1 %fusion.1 = f32[12,512]{1,0:T(8,128)S(1)} fusion(f32[12,512,2048]{2,1,0:T(8,128)} %get-tuple-element.13, f32[12,512]{1,0:T(8,128)S(1)} %broadcast_maximum_fusion, pred[2048]{0:T(1024)(128)(4,1)S(1)} %broadcast_bitcast_fusion), kind=kLoop, calls=%fused_computation.4 | loop fusion | flops 50325504 | bytes 50382848 | tf_op jit(solution)/shard_map/reduce_sum | solution.py:52
  119.2 0.8 copy.27
  120.0 0.0 reduce-scatter.12.cloned.1.call-update
  120.0 0.0 reduce-scatter.10.cloned.1.call-start
  120.1 22.0 %fusion.7 = bf16[512,12,128]{0,2,1:T(8,128)(2,1)S(1)} fusion(bf16[2048,12,128]{0,2,1:T(8,128)(2,1)} %bitcast.49, f32[12,512,2048]{2,1,0:T(8,128)} %get-tuple-element.13, f32[12,512]{1,0:T(8,128)S(1)} %broadcast_maximum_fusion, pred[2048]{0:T(1024)(128)(4,1)S(1)} %broadcast_bitcast_fusion, f32[512,12]{0,1:T(8,128)S(1)} %get-tuple-element.10, ...), kind=kOutput, calls=%fused_computation.11 | convolution fusion | flops 3273916416 | bytes 58271744 | tf_op jit(solution)/shard_map/hqk,khd->qhd/dot_general | solution.py:53
  142.1 1.6 copy.25
  143.7 0.2 reduce-scatter.8.cloned.1.call-start
  143.9 0.0 reduce-scatter.12.cloned.1.call-done
  144.0 0.8 copy.28
  144.8 32.3 %reduce-scatter.10.cloned.1.call-done = bf16[128,1536]{1,0:T(8,128)(2,1)} async-done(((bf16[512,1536]{1,0:T(8,128)(2,1)}), bf16[128,1536]{1,0:T(8,128)(2,1)}) %reduce-scatter.10.cloned.1.call-update) | async-done | bytes 393232
  177.1 1.2 copy.26
  178.3 0.1 fusion.10
  178.4 10.3 %convolution_convert_fusion = bf16[128,6144]{1,0:T(8,128)(2,1)} fusion(bf16[128,1536]{0,1:T(8,128)(2,1)S(1)} %fusion.10, bf16[1536,6144]{1,0:T(8,128)(2,1)} %param.9), kind=kOutput, calls=%fused_computation.8 | convolution fusion | flops 2416705536 | bytes 20840448 | tf_op jit(solution)/shard_map/dot_general | solution.py:75
  188.6 27.3 %reduce-scatter.8.cloned.1.call-done = bf16[32,6144]{1,0:T(8,128)(2,1)} async-done(((bf16[128,6144]{1,0:T(8,128)(2,1)}), bf16[32,6144]{1,0:T(8,128)(2,1)}) %reduce-scatter.8.cloned.1.call-update) | async-done | bytes 393232 | tf_op jit(solution)/shard_map/reduce_scatter | solution.py:74
  (16 shorter events, 0.1 us)
Async XLA Ops:
  6.5 29.7 %copy-start = (s32[16]{0:T(128)S(1)}, s32[16]{0:T(128)}, u32[]{:S(2)}) copy-start(s32[16]{0:T(128)} %param.8) | copy-start | bytes 196
  6.5 51.4 %all-gather.2.cloned.1.call-start = ((), (), s32[]{:S(2)}) async-start(), calls=%async_computation.3 | async-start | bytes 1966080 | tf_op jit(solution)/shard_map/all_gather | solution.py:37
  8.7 3.3 %collective-permute-start = (bf16[32,1536]{1,0:T(8,128)(2,1)S(1)}, bf16[32,1536]{1,0:T(8,128)(2,1)S(1)}, u32[]{:S(2)}, u32[]{:S(2)}) collective-permute-start(bf16[32,1536]{1,0:T(8,128)(2,1)S(1)} %bitcast.58), channel_id=1, source_target_pairs={{0,4},{4,0},{8,12},{12,8},{1,5},{5,1},{9,13},{13,9},{2,6},{6,2},{1... | collective-permute-start | bytes 294920 | tf_op jit(solution)/shard_map/ppermute | solution.py:34
  9.2 6.2 %collective-permute-start.1 = (bf16[32,1536]{1,0:T(8,128)(2,1)S(1)}, bf16[32,1536]{1,0:T(8,128)(2,1)S(1)}, u32[]{:S(2)}, u32[]{:S(2)}) collective-permute-start(bf16[32,1536]{1,0:T(8,128)(2,1)S(1)} %bitcast.59), channel_id=1, source_target_pairs={{0,8},{4,12},{8,0},{12,4},{1,9},{5,13},{9,1},{13,5},{2,10},{6,14},... | collective-permute-start | bytes 294920 | tf_op jit(solution)/shard_map/ppermute | solution.py:34
  11.8 5.3 %collective-permute-start.2 = (bf16[32,1536]{1,0:T(8,128)(2,1)S(1)}, bf16[32,1536]{1,0:T(8,128)(2,1)S(1)}, u32[]{:S(2)}, u32[]{:S(2)}) collective-permute-start(bf16[32,1536]{1,0:T(8,128)(2,1)S(1)} %bitcast.60), channel_id=1, source_target_pairs={{0,12},{4,8},{8,4},{12,0},{1,13},{5,9},{9,5},{13,1},{2,14},{6,10},... | collective-permute-start | bytes 294920 | tf_op jit(solution)/shard_map/ppermute | solution.py:34
  18.7 125.2 %reduce-scatter.12.cloned.1.call-start = ((), (), s32[]{:S(2)}) async-start(), calls=%async_computation.6 | async-start | bytes 163840
  120.0 57.0 %reduce-scatter.10.cloned.1.call-start = ((), (), s32[]{:S(2)}) async-start(), calls=%async_computation.5 | async-start | bytes 1966080
  143.7 72.2 %reduce-scatter.8.cloned.1.call-start = ((), (), s32[]{:S(2)}) async-start(), calls=%async_computation.4 | async-start | bytes 1966080 | tf_op jit(solution)/shard_map/reduce_scatter | solution.py:74
Sparse Core Ops, SparseCore 0:
  18.9 38.9 all-gather.1
  120.1 17.1 reduce-scatter.11
  143.8 33.1 reduce-scatter.9
  188.8 27.1 reduce-scatter.7
